TPU v7x, 32 devices: a whole 2x2x4 slice. The times are simulated.
32 devices in a mesh: snode: 8 (over z, x), col: 4 (over y, core).
Axes of the slice: x: 2, y: 2, z: 4, core: 2. Of those that a mesh axis runs over, the one named last changes fastest.
Arguments:
- rhs: float32 [3, 8192, 256], P(None, ('snode', 'col')), may hold values from -6 to 6
- dinv: bfloat16 [3, 8192, 1024], P(None, ('snode', 'col')), may hold values from -2 to 2, as said below
- loff: bfloat16 [2, 65536, 1024], P(None, ('snode', 'col')), may hold values from -0.046875 to 0.046875
- targets: int32 [2, 512], P(None, ('snode', 'col')), may hold values from 0 to 15, as said below
Outputs:
- solution: float32 [3, 8192, 256], P(None, ('snode', 'col'))
Inputs may be any that keep to these rules, and one draw needn't show every extreme that they name: `targets`: the 16 entries that one device holds for one level are distinct. `dinv`: each block is the inverse of a lower-triangular block: lower triangular, with diagonal entries from 0.5 to 2.
All inputs are finite; a program needn't handle non-finite values.
Results may differ from a plain program's by a relative error of at most 0.025.
Values may be sent and summed in bfloat16 or wider, within the bound.
A program may use at most 64 MiB of HBM per device.

v0:
```python
import jax
import jax.numpy as jnp
from jax import lax
from jax.experimental import pallas as pl
from jax.experimental.pallas import tpu as pltpu
from jax.sharding import PartitionSpec as P

BLK = 128


def solve_block(matrix, resid_bf):
    return jnp.dot(
        matrix,
        lax.all_gather(resid_bf, "col", axis=0, tiled=True),
        preferred_element_type=jnp.float32,
    )


def route(update, links, col_rows):
    groups = lax.axis_size("snode")
    rhs_count = update.shape[1]
    flat = update.reshape(links.shape[0], BLK * rhs_count)
    count = groups * col_rows
    number = count // BLK
    wanted = 0 // BLK + lax.iota(jnp.int32, number)
    select = (wanted[:, None] == links[None, :]).astype(jnp.bfloat16)
    outgoing = (
        jnp.dot(select, flat, preferred_element_type=jnp.float32)
        .reshape(count, rhs_count)
        .astype(jnp.bfloat16)
        .reshape(groups, col_rows, rhs_count)
    )
    arrived = lax.all_to_all(outgoing, "snode", split_axis=0, concat_axis=0, tiled=True)
    return jnp.sum(arrived.astype(jnp.float32), axis=0)


def fetch(upper_bf, links):
    rhs_count = upper_bf.shape[1]
    gathered = lax.all_gather(upper_bf, "snode", axis=0, tiled=True)
    number = gathered.shape[0] // BLK
    wanted = lax.iota(jnp.int32, number)
    select = (links[:, None] == wanted[None, :]).astype(jnp.bfloat16)
    picked = jnp.dot(
        select, gathered.reshape(number, BLK * rhs_count), preferred_element_type=jnp.float32
    )
    return picked.astype(jnp.bfloat16).reshape(links.shape[0] * BLK, rhs_count)


def back_term(blocks, picked, col_rows):
    contract = (((0,), (0,)), ((), ()))

    def term(start, count):
        return lax.dot_general(blocks, picked, contract, preferred_element_type=jnp.float32)

    return lax.psum_scatter(
        term(jnp.int32(0), col_rows * lax.axis_size("col")).astype(jnp.bfloat16),
        "col",
        scatter_dimension=0,
        tiled=True,
    ).astype(jnp.float32)


def back_solve(matrix, reduced_bf, col_rows):
    contract = (((0,), (0,)), ((), ()))

    def term(start, count):
        return lax.dot_general(matrix, reduced_bf, contract, preferred_element_type=jnp.float32)

    return lax.psum_scatter(
        term(jnp.int32(0), col_rows * lax.axis_size("col")).astype(jnp.bfloat16),
        "col",
        scatter_dimension=0,
        tiled=True,
    ).astype(jnp.float32)


def body(rhs, dinv, loff, targets):
    levels = rhs.shape[0]
    col_rows = rhs.shape[1]
    rhs_count = rhs.shape[2]
    incoming = jnp.zeros((col_rows, rhs_count), jnp.float32)
    forward = []
    for level in range(levels):
        resid_bf = (rhs[level] - incoming).astype(jnp.bfloat16)
        solved = solve_block(dinv[level], resid_bf)
        forward.append(solved)
        if level + 1 < levels:
            solved_bf = solved.astype(jnp.bfloat16)
            full_bf = lax.all_gather(solved_bf, "col", axis=0, tiled=True)
            update = jnp.dot(loff[level], full_bf, preferred_element_type=jnp.float32).astype(
                jnp.bfloat16
            )
            incoming = route(update, targets[level], col_rows)
    outputs = [None] * levels
    upper_bf = None
    for level in reversed(range(levels)):
        reduced = forward[level]
        if level + 1 < levels:
            picked = fetch(upper_bf, targets[level])
            reduced = reduced - back_term(loff[level], picked, col_rows)
        solved = back_solve(dinv[level], reduced.astype(jnp.bfloat16), col_rows)
        outputs[level] = solved
        upper_bf = solved.astype(jnp.bfloat16)
    return jnp.stack(outputs)


NZ = 4
MESH_ID = pl.DeviceIdType.MESH
SENDS = 112
OFFSET = 0.0


def dot32(a, b):
    return jnp.dot(a, b, preferred_element_type=jnp.float32)


def fused_kernel(
    targets_ref,
    rhs_hbm,
    dinv_hbm,
    loff_hbm,
    out_hbm,
    rhs_v,
    d_v,
    loff_0,
    loff_1,
    r_v,
    f_v,
    fwd_own,
    fwd_all,
    own_u,
    xsend,
    xrecv,
    zsend,
    zrecv,
    up_v,
    upx_v,
    acc,
    csend,
    crecv,
    ysend,
    yrecv,
    out_v,
    inv_ref,
    local_sem,
    send_sem,
    recv_sem,
):
    bf = jnp.bfloat16
    rows = rhs_v.shape[1]
    half = r_v.shape[4]
    width = d_v.shape[3]
    s = lax.axis_index("snode")
    c = lax.axis_index("col")
    z, x = lax.div(s, 2), lax.rem(s, 2)
    y, k = lax.div(c, 2), lax.rem(c, 2)
    c_y = (1 - y) * 2 + k
    c_core = y * 2 + 1 - k
    c_diag = (1 - y) * 2 + 1 - k
    y_peer = (s, c_y)
    core_peer = (s, c_core)
    x_peer = (z * 2 + 1 - x, c)

    def z_at(d):
        return lax.rem(z + d, NZ)

    def z_peer(d):
        return (z_at(d) * 2 + x, c)

    loads = []

    def load(src, dst):
        copy = pltpu.make_async_copy(src, dst, local_sem.at[len(loads)])
        copy.start()
        loads.append(copy)
        return copy

    load_rhs = load(rhs_hbm, rhs_v)
    load_d = [None] * 3
    load_loff = [None] * 2
    load_d[0] = load(dinv_hbm.at[0], d_v.at[0, c])
    load_loff[0] = load(loff_hbm.at[0], loff_0)
    load_d[1] = load(dinv_hbm.at[1], d_v.at[1, c])
    load_loff[1] = load(loff_hbm.at[1], loff_1)
    load_d[2] = load(dinv_hbm.at[2], d_v.at[2, c])

    barrier = pltpu.get_barrier_semaphore()
    peers = [y_peer, core_peer, x_peer, z_peer(1), z_peer(2), z_peer(3)]
    for peer in peers:
        pl.semaphore_signal(barrier, inc=1, device_id=peer, device_id_type=MESH_ID)
    load_rhs.wait()
    for h in range(2):
        r_v[h, 0, c] = rhs_v[0, :, h * half : (h + 1) * half].astype(bf)
    pl.semaphore_wait(barrier, len(peers))

    sent = []
    stores = []

    def remote(src, dst, peer):
        at = len(sent)
        copy = pltpu.make_async_remote_copy(
            src_ref=src,
            dst_ref=dst,
            send_sem=send_sem.at[at],
            recv_sem=recv_sem.at[at],
            device_id=peer,
            device_id_type=MESH_ID,
        )
        copy.start()
        sent.append(copy)
        return copy

    def gather_start(buf):
        to_y = remote(buf.at[c], buf.at[c], y_peer)
        to_core = remote(buf.at[c], buf.at[c], core_peer)
        return to_y, to_core

    def gather_relay(buf, started):
        started[0].wait_recv()
        return remote(buf.at[c_y], buf.at[c_y], core_peer)

    def gather_end(started, relay):
        started[1].wait_recv()
        relay.wait_recv()

    def full(buf):
        return buf[...].reshape(4 * rows, half)

    def invert():
        links = inv_ref.shape[1]
        for level in range(2):
            entries = [targets_ref[level, at] for at in range(links)]
            for row in range(links):
                found = jnp.int32(0)
                for at, entry in enumerate(entries):
                    found = jnp.where(entry == row, jnp.int32(at), found)
                inv_ref[level, row] = found

    def link_rows(level, zt, xt):
        group = (zt * 2 + xt) * 2
        loff_v = (loff_0, loff_1)[level]
        first = loff_v[inv_ref[level, group]]
        second = loff_v[inv_ref[level, group + 1]]
        return jnp.concatenate([first, second], axis=0)

    def columns(level, index):
        at = pl.multiple_of(index * rows, rows)
        return d_v[level, :, :, pl.ds(at, rows)].reshape(width, rows)

    order = (2, 1, 3, 0)
    shared = {}

    def chain(h):
        lead = h == 0
        f32 = jnp.float32
        lanes = slice(h * half, (h + 1) * half)

        def gather(buf, started):
            yield 4.1
            relay = gather_relay(buf, started)
            yield 1.1
            gather_end(started, relay)

        def route_sum(level, fwd_bf):
            arrivals = {}
            for d in order:
                part = dot32(link_rows(level, z_at(d), 1 - x), fwd_bf)
                xsend[h, level, d] = part.astype(bf)
                arrivals[d] = remote(xsend.at[h, level, d], xrecv.at[h, level, d], x_peer)
            for d in order:
                own_u[h, d] = dot32(link_rows(level, z_at(d), x), fwd_bf)
            landed = []
            for d in order[:3]:
                yield 1.0
                arrivals[d].wait_recv()
                both = own_u[h, d] + xrecv[h, level, d].astype(f32)
                zsend[h, level, d] = both.astype(bf)
                landed.append(
                    remote(zsend.at[h, level, d], zrecv.at[h, level, d], z_peer(d))
                )
            yield 1.0
            arrivals[0].wait_recv()
            total = own_u[h, 0] + xrecv[h, level, 0].astype(f32)
            for at, d in enumerate(order[:3]):
                yield 3.0 if at == 0 else 1.0
                landed[at].wait_recv()
                total = total + zrecv[h, level, d].astype(f32)
            r_v[h, level + 1, c] = (rhs_v[level + 1, :, lanes] - total).astype(bf)

        started = gather_start(r_v.at[h, 0])
        if lead:
            load_d[0].wait()
            invert()
        yield from gather(r_v.at[h, 0], started)
        own = dot32(d_v[0, c], full(r_v.at[h, 0]))
        fwd_own[h, 0] = own
        f_v[h, 0, c] = own.astype(bf)
        started = gather_start(f_v.at[h, 0])
        if lead:
            load_loff[0].wait()
            load_d[1].wait()
        yield from gather(f_v.at[h, 0], started)
        if lead:
            shared[1] = gather_start(d_v.at[1])
        yield from route_sum(0, full(f_v.at[h, 0]))

        started = gather_start(r_v.at[h, 1])
        if lead:
            d_relay = gather_relay(d_v.at[1], shared[1])
        yield from gather(r_v.at[h, 1], started)
        if lead:
            gather_end(shared[1], d_relay)
        for i in range(4):
            part = dot32(d_v[1, i], full(r_v.at[h, 1]))
            fwd_all[h, i] = part
            f_v[h, 1, i] = part.astype(bf)
        if lead:
            load_d[2].wait()
            load_loff[1].wait()
            shared[2] = gather_start(d_v.at[2])
        yield from route_sum(1, full(f_v.at[h, 1]))

        started = gather_start(r_v.at[h, 2])
        if lead:
            d_relay = gather_relay(d_v.at[2], shared[2])
        fwd_own[h, 1] = fwd_all[h, c]
        yield from gather(r_v.at[h, 2], started)
        if lead:
            gather_end(shared[2], d_relay)
            shared[0] = gather_start(d_v.at[0])
        for i in range(4):
            f_v[h, 2, i] = dot32(d_v[2, i], full(r_v.at[h, 2])).astype(bf)

        def finish(level, sol_t):
            out_v[h, level] = sol_t.T
            copy = pltpu.make_async_copy(
                out_v.at[h, level],
                out_hbm.at[level, :, pl.ds(h * half, half)],
                local_sem.at[6 + 2 * level + h],
            )
            copy.start()
            stores.append(copy)

        sol_t = lax.dot_general(
            full(f_v.at[h, 2]),
            columns(2, c),
            (((0,), (0,)), ((), ())),
            preferred_element_type=f32,
        )
        for level in (1, 0):
            up_v[h, level, 0] = sol_t.astype(bf)
            own_up = up_v.at[h, level, 0]
            from_z = {}
            from_x = {0: remote(own_up, upx_v.at[h, level, 0], x_peer)}
            for d in (2, 1, 3):
                from_z[d] = remote(own_up, up_v.at[h, level, d], z_peer(d))
            finish(level + 1, sol_t)
            acc[h] = jnp.zeros((half, width), f32)
            at = pl.multiple_of(c * rows, rows)
            acc[h, :, pl.ds(at, rows)] = -(fwd_own[h, level].T)
            acc[h] += dot32(up_v[h, level, 0], link_rows(level, z, x))
            for step, d in enumerate((1, 3, 2)):
                yield 4.5 if step == 0 else 1.4
                from_z[d].wait_recv()
                from_x[d] = remote(up_v.at[h, level, d], upx_v.at[h, level, d], x_peer)
                acc[h] += dot32(up_v[h, level, d], link_rows(level, z_at(NZ - d), x))
            for d in (0, 1, 3, 2):
                yield 2.5 if d == 2 else 0.7
                from_x[d].wait_recv()
                acc[h] += dot32(upx_v[h, level, d], link_rows(level, z_at(NZ - d), 1 - x))
            if lead and level == 1:
                shared["relay"] = gather_relay(d_v.at[0], shared[0])
            if lead and level == 0:
                gather_end(shared[0], shared["relay"])
            v_bf = acc[h].astype(bf)
            csend[h, level, 0] = dot32(v_bf, columns(level, c_diag)).astype(bf)
            far = remote(csend.at[h, level, 0], crecv.at[h, level, 0], core_peer)
            csend[h, level, 1] = dot32(v_bf, columns(level, c_core)).astype(bf)
            near = remote(csend.at[h, level, 1], crecv.at[h, level, 1], core_peer)
            mine = dot32(v_bf, columns(level, c_y))
            yield 0.5
            far.wait_recv()
            ysend[h, level] = (mine + crecv[h, level, 0].astype(f32)).astype(bf)
            across = remote(ysend.at[h, level], yrecv.at[h, level], y_peer)
            mine = dot32(v_bf, columns(level, c))
            near.wait_recv()
            mine = mine + crecv[h, level, 1].astype(f32)
            yield 3.5
            across.wait_recv()
            sol_t = -(mine + yrecv[h, level].astype(f32))
        finish(0, sol_t)

    chains = [chain(0), chain(1)]
    ready = [0.0, OFFSET]
    steps = [0, 0]
    now = 0.0
    running = {0, 1}
    while running:
        pick = min(running, key=lambda h: (ready[h], h))
        if pick == 1 and 0 in running and steps[1] >= steps[0]:
            pick = 0
        now = max(now, ready[pick]) + 0.4
        steps[pick] += 1
        try:
            ready[pick] = now + next(chains[pick])
        except StopIteration:
            running.discard(pick)
    for copy in sent:
        copy.wait_send()
    for copy in stores:
        copy.wait()


def fused_body(rhs, dinv, loff, targets):
    levels, rows, count = rhs.shape
    width = dinv.shape[2]
    links = targets.shape[1]
    bf = jnp.bfloat16
    f32 = jnp.float32
    any_space = pl.BlockSpec(memory_space=pl.ANY)
    blk = (rows, count // 2)
    blk_t = (count // 2, rows)
    return pl.pallas_call(
        fused_kernel,
        out_shape=jax.ShapeDtypeStruct(rhs.shape, f32),
        in_specs=[pl.BlockSpec(memory_space=pltpu.SMEM), any_space, any_space, any_space],
        out_specs=any_space,
        scratch_shapes=[
            pltpu.VMEM((levels, rows, count), f32),
            pltpu.VMEM((levels, 4, rows, width), bf),
            pltpu.VMEM((links, BLK, width), bf),
            pltpu.VMEM((links, BLK, width), bf),
            pltpu.VMEM((2, levels, 4) + blk, bf),
            pltpu.VMEM((2, levels, 4) + blk, bf),
            pltpu.VMEM((2, 2) + blk, f32),
            pltpu.VMEM((2, 4) + blk, f32),
            pltpu.VMEM((2, 4) + blk, f32),
            pltpu.VMEM((2, 2, 4) + blk, bf),
            pltpu.VMEM((2, 2, 4) + blk, bf),
            pltpu.VMEM((2, 2, 4) + blk, bf),
            pltpu.VMEM((2, 2, 4) + blk, bf),
            pltpu.VMEM((2, 2, 4) + blk_t, bf),
            pltpu.VMEM((2, 2, 4) + blk_t, bf),
            pltpu.VMEM((2, count // 2, width), f32),
            pltpu.VMEM((2, 2, 2) + blk_t, bf),
            pltpu.VMEM((2, 2, 2) + blk_t, bf),
            pltpu.VMEM((2, 2) + blk_t, bf),
            pltpu.VMEM((2, 2) + blk_t, bf),
            pltpu.VMEM((2, levels) + blk, f32),
            pltpu.SMEM((levels - 1, links), jnp.int32),
            pltpu.SemaphoreType.DMA((12,)),
            pltpu.SemaphoreType.DMA((SENDS,)),
            pltpu.SemaphoreType.DMA((SENDS,)),
        ],
        compiler_params=pltpu.CompilerParams(
            collective_id=0, has_side_effects=True, vmem_limit_bytes=60 * 1024 * 1024
        ),
    )(targets, rhs, dinv, loff.reshape(levels - 1, links, BLK, width))


def solution(mesh):
    in_specs = (
        P(None, ("snode", "col"), None),
        P(None, ("snode", "col"), None),
        P(None, ("snode", "col"), None),
        P(None, ("snode", "col")),
    )
    out_specs = P(None, ("snode", "col"), None)
    fits = mesh.shape["snode"] == 2 * NZ and mesh.shape["col"] == 4
    return jax.shard_map(
        fused_body if fits else body,
        mesh=mesh,
        in_specs=in_specs,
        out_specs=out_specs,
        check_vma=False,
    )
```

profile of v0, /device:TPU:16, one launch (start us, length us, event | category | flops | bytes accessed | tf_op | source)
XLA Modules:
  0.0 115.8 jit_solution(6189034669237864580)
XLA Ops:
  0.0 113.8 %shard_map.46 = f32[3,256,256]{2,1,0:T(8,128)} custom-call(s32[2,16]{1,0:T(2,128)} %targets_ref.1, f32[3,256,256]{2,1,0:T(8,128)} %rhs_hbm.1, bf16[3,256,1024]{2,1,0:T(8,128)(2,1)} %dinv_hbm.1, bf16[2,16,128,1024]{3,2,1,0:T(8,128)(2,1)} %bitcast.1), custom_call_target="tpu_custom_call" | custom-call | tf_op jit(solution)/shard_map/pallas_call | solution.py:423
  113.8 2.1 %copy.6 = f32[3,256,256]{2,1,0:T(8,128)} copy(f32[3,256,256]{2,1,0:T(8,128)} %shard_map.46) | data formatting | bytes 1572864
where the time goes:
time: 116 us
  Pallas kernels  114 us (98%)
  local copies, waits for them, and re-layouts  2.06 us (2%)
    pallas_call x1, Pallas kernels, fused_body(): pl.pallas_call(fused_kernel, out_shape=jax.ShapeDtypeStruct(rhs.shape, f3...  114 us

commit v1 on v0

--- a/solution.py
+++ b/solution.py
@@ -107,7 +107,7 @@
 NZ = 4
 MESH_ID = pl.DeviceIdType.MESH
 SENDS = 112
-OFFSET = 0.0
+OFFSET = 3.0
 
 
 def dot32(a, b):

time: 116 us -> 103 us (0.89)
  Pallas kernels: 114 us -> 101 us
    pallas_call x1, Pallas kernels: 114 us -> 101 us  [fused_body(): pl.pallas_call(fused_kernel, out_shape=jax.ShapeDtypeStruct(rhs.shape, f3...]
where the time goes in v1:
time: 103 us
  Pallas kernels  101 us (98%)
  local copies, waits for them, and re-layouts  2.06 us (2%)
    pallas_call x1, Pallas kernels, fused_body(): pl.pallas_call(fused_kernel, out_shape=jax.ShapeDtypeStruct(rhs.shape, f3...  101 us
    unnamed x1, local copies, waits for them, and re-layouts  2.06 us

profile of v1, /device:TPU:16, one launch (start us, length us, event | category | flops | bytes accessed | tf_op | source)
XLA Modules:
  0.0 102.7 jit_solution(12771834023889529356)
XLA Ops:
  0.0 100.7 %shard_map.46 = f32[3,256,256]{2,1,0:T(8,128)} custom-call(s32[2,16]{1,0:T(2,128)} %targets_ref.1, f32[3,256,256]{2,1,0:T(8,128)} %rhs_hbm.1, bf16[3,256,1024]{2,1,0:T(8,128)(2,1)} %dinv_hbm.1, bf16[2,16,128,1024]{3,2,1,0:T(8,128)(2,1)} %bitcast.1), custom_call_target="tpu_custom_call" | custom-call | tf_op jit(solution)/shard_map/pallas_call | solution.py:423
  100.7 2.1 %copy.6 = f32[3,256,256]{2,1,0:T(8,128)} copy(f32[3,256,256]{2,1,0:T(8,128)} %shard_map.46) | data formatting | bytes 1572864

commit v2 on v1

v2 whole, which is shorter than its diff:
```python
import jax
import jax.numpy as jnp
from jax import lax
from jax.experimental import pallas as pl
from jax.experimental.pallas import tpu as pltpu
from jax.sharding import PartitionSpec as P

BLK = 128


def solve_block(matrix, resid_bf):
    return jnp.dot(
        matrix,
        lax.all_gather(resid_bf, "col", axis=0, tiled=True),
        preferred_element_type=jnp.float32,
    )


def route(update, links, col_rows):
    groups = lax.axis_size("snode")
    rhs_count = update.shape[1]
    flat = update.reshape(links.shape[0], BLK * rhs_count)
    count = groups * col_rows
    number = count // BLK
    wanted = 0 // BLK + lax.iota(jnp.int32, number)
    select = (wanted[:, None] == links[None, :]).astype(jnp.bfloat16)
    outgoing = (
        jnp.dot(select, flat, preferred_element_type=jnp.float32)
        .reshape(count, rhs_count)
        .astype(jnp.bfloat16)
        .reshape(groups, col_rows, rhs_count)
    )
    arrived = lax.all_to_all(outgoing, "snode", split_axis=0, concat_axis=0, tiled=True)
    return jnp.sum(arrived.astype(jnp.float32), axis=0)


def fetch(upper_bf, links):
    rhs_count = upper_bf.shape[1]
    gathered = lax.all_gather(upper_bf, "snode", axis=0, tiled=True)
    number = gathered.shape[0] // BLK
    wanted = lax.iota(jnp.int32, number)
    select = (links[:, None] == wanted[None, :]).astype(jnp.bfloat16)
    picked = jnp.dot(
        select, gathered.reshape(number, BLK * rhs_count), preferred_element_type=jnp.float32
    )
    return picked.astype(jnp.bfloat16).reshape(links.shape[0] * BLK, rhs_count)


def back_term(blocks, picked, col_rows):
    contract = (((0,), (0,)), ((), ()))

    def term(start, count):
        return lax.dot_general(blocks, picked, contract, preferred_element_type=jnp.float32)

    return lax.psum_scatter(
        term(jnp.int32(0), col_rows * lax.axis_size("col")).astype(jnp.bfloat16),
        "col",
        scatter_dimension=0,
        tiled=True,
    ).astype(jnp.float32)


def back_solve(matrix, reduced_bf, col_rows):
    contract = (((0,), (0,)), ((), ()))

    def term(start, count):
        return lax.dot_general(matrix, reduced_bf, contract, preferred_element_type=jnp.float32)

    return lax.psum_scatter(
        term(jnp.int32(0), col_rows * lax.axis_size("col")).astype(jnp.bfloat16),
        "col",
        scatter_dimension=0,
        tiled=True,
    ).astype(jnp.float32)


def body(rhs, dinv, loff, targets):
    levels = rhs.shape[0]
    col_rows = rhs.shape[1]
    rhs_count = rhs.shape[2]
    incoming = jnp.zeros((col_rows, rhs_count), jnp.float32)
    forward = []
    for level in range(levels):
        resid_bf = (rhs[level] - incoming).astype(jnp.bfloat16)
        solved = solve_block(dinv[level], resid_bf)
        forward.append(solved)
        if level + 1 < levels:
            solved_bf = solved.astype(jnp.bfloat16)
            full_bf = lax.all_gather(solved_bf, "col", axis=0, tiled=True)
            update = jnp.dot(loff[level], full_bf, preferred_element_type=jnp.float32).astype(
                jnp.bfloat16
            )
            incoming = route(update, targets[level], col_rows)
    outputs = [None] * levels
    upper_bf = None
    for level in reversed(range(levels)):
        reduced = forward[level]
        if level + 1 < levels:
            picked = fetch(upper_bf, targets[level])
            reduced = reduced - back_term(loff[level], picked, col_rows)
        solved = back_solve(dinv[level], reduced.astype(jnp.bfloat16), col_rows)
        outputs[level] = solved
        upper_bf = solved.astype(jnp.bfloat16)
    return jnp.stack(outputs)


NZ = 4
MESH_ID = pl.DeviceIdType.MESH
SENDS = 96
ZS = (2, 1, 3)
STEPS = tuple((d, kk) for kk in range(2) for d in (2, 1, 3))
RSO = (2, 1, 3, 0)


def dot32(a, b):
    return jnp.dot(a, b, preferred_element_type=jnp.float32)


def fused_kernel(
    targets_ref,
    targets_hbm,
    rhs_hbm,
    dinv_hbm,
    loff_hbm,
    out_hbm,
    rhs_0,
    rhs_v,
    d_v,
    loff_0,
    loff_1,
    r_v,
    f_v,
    stage,
    fwd_own,
    own_u,
    xsend,
    xrecv,
    zsend,
    zrecv,
    up_v,
    upx_v,
    acc,
    ysend,
    yrecv,
    out_v,
    peer_links_v,
    peer_links,
    inv_ref,
    local_sem,
    send_sem,
    recv_sem,
):
    bf = jnp.bfloat16
    f32 = jnp.float32
    rows = rhs_0.shape[0]
    half = r_v.shape[3]
    width = d_v.shape[3]
    s = lax.axis_index("snode")
    c = lax.axis_index("col")
    z, x = lax.div(s, 2), lax.rem(s, 2)
    y, k = lax.div(c, 2), lax.rem(c, 2)
    c_y = (1 - y) * 2 + k
    c_core = y * 2 + 1 - k
    y_peer = (s, c_y)
    core_peer = (s, c_core)
    diag_peer = (s, (1 - y) * 2 + 1 - k)
    x_peer = (z * 2 + 1 - x, c)
    own = pl.ds(y * 2, 2)
    lanes = pl.ds(pl.multiple_of(k * half, half), half)
    other = pl.ds(pl.multiple_of((1 - k) * half, half), half)

    def z_at(d):
        return lax.rem(z + d, NZ)

    def z_peer(d):
        return (z_at(d) * 2 + x, c)

    loads = {}
    waited = set()

    def load(name, src, dst):
        copy = pltpu.make_async_copy(src, dst, local_sem.at[len(loads)])
        copy.start()
        loads[name] = copy

    def need(*names):
        for name in names:
            if name not in waited:
                waited.add(name)
                if name in loads:
                    loads[name].wait()
                else:
                    pushed[name].wait_recv()

    load("rhs0", rhs_hbm.at[0], rhs_0)
    load("d0", dinv_hbm.at[0], d_v.at[0, c])
    load("loff0", loff_hbm.at[0], loff_0.at[k])
    load("d1", dinv_hbm.at[1], d_v.at[1, c])
    load("rhs1", rhs_hbm.at[1, :, lanes], rhs_v.at[0, k])
    load("rhs2", rhs_hbm.at[2, :, lanes], rhs_v.at[1, k])
    load("loff1", loff_hbm.at[1], loff_1.at[k])
    load("d2", dinv_hbm.at[2], d_v.at[2, c])

    barrier = pltpu.get_barrier_semaphore()
    peers = [y_peer, core_peer, diag_peer, x_peer, z_peer(1), z_peer(2), z_peer(3)]
    for peer in peers:
        pl.semaphore_signal(barrier, inc=1, device_id=peer, device_id_type=MESH_ID)
    need("rhs0")
    r_v[0, c] = rhs_0[:, lanes].astype(bf)
    stage[...] = rhs_0[:, other].astype(bf)
    pl.semaphore_wait(barrier, len(peers))

    sent = []
    pushed = {}

    def describe(src, dst, peer):
        at = len(sent)
        copy = pltpu.make_async_remote_copy(
            src_ref=src,
            dst_ref=dst,
            send_sem=send_sem.at[at],
            recv_sem=recv_sem.at[at],
            device_id=peer,
            device_id_type=MESH_ID,
        )
        sent.append(copy)
        return copy

    def remote(src, dst, peer):
        copy = describe(src, dst, peer)
        copy.start()
        return copy

    def push(name, src, dst):
        pushed[name] = remote(src, dst, core_peer)

    def to_y(buf, kk):
        return remote(buf.at[y * 2 + kk], buf.at[y * 2 + kk], y_peer)

    def full(buf):
        return buf[...].reshape(4 * rows, half)

    def invert(level, kk, source):
        links = inv_ref.shape[2]
        entries = [source[level, at] for at in range(links)]
        for row in range(links):
            found = jnp.int32(0)
            for at, entry in enumerate(entries):
                found = jnp.where(entry == row, jnp.int32(at), found)
            inv_ref[level, kk, row] = found

    def link_rows(level, kk, zt, xt):
        group = (zt * 2 + xt) * 2
        loff_v = (loff_0, loff_1)[level]
        first = loff_v[kk, inv_ref[level, kk, group]]
        second = loff_v[kk, inv_ref[level, kk, group + 1]]
        return jnp.concatenate([first, second], axis=0)

    def columns(level, index):
        at = pl.multiple_of(index * rows, rows)
        return d_v[level, :, :, pl.ds(at, rows)].reshape(width, rows)

    first = [
        remote(r_v.at[0, c], r_v.at[0, c], y_peer),
        remote(stage, r_v.at[0, c], diag_peer),
        remote(stage, r_v.at[0, c], core_peer),
    ]
    push("d0c", dinv_hbm.at[0], d_v.at[0, c])
    push("links", targets_hbm, peer_links_v)
    push("loff0c", loff_hbm.at[0], loff_0.at[k])
    push("d1c", dinv_hbm.at[1], d_v.at[1, c])
    push("rhs1c", rhs_hbm.at[1, :, other], rhs_v.at[0, k])
    push("rhs2c", rhs_hbm.at[2, :, other], rhs_v.at[1, k])
    push("loff1c", loff_hbm.at[1], loff_1.at[k])
    push("d2c", dinv_hbm.at[2], d_v.at[2, c])

    d_y = {}
    d_relay = {}
    for level in (1, 2, 0):
        d_y[level] = describe(d_v.at[level, c], d_v.at[level, c], y_peer)
        d_relay[level] = describe(d_v.at[level, c_y], d_v.at[level, c_y], core_peer)

    def relay_d(level):
        d_y[level].wait_recv()
        d_relay[level].start()

    for level in range(2):
        invert(level, k, targets_ref)
    need("links")
    copy = pltpu.make_async_copy(peer_links_v, peer_links, local_sem.at[15])
    copy.start()
    copy.wait()
    for level in range(2):
        invert(level, 1 - k, peer_links)

    order = RSO

    def route_sum(level, fwd_bf):
        arrivals = {}
        for d in order:
            for kk in range(2):
                part = dot32(link_rows(level, kk, z_at(d), 1 - x), fwd_bf)
                xsend[level, d, kk] = part.astype(bf)
                arrivals[d, kk] = remote(
                    xsend.at[level, d, kk], xrecv.at[level, d, kk], x_peer
                )
        for d in order:
            for kk in range(2):
                own_u[d, kk] = dot32(link_rows(level, kk, z_at(d), x), fwd_bf)
        landed = {}
        for d in order[:3]:
            for kk in range(2):
                arrivals[d, kk].wait_recv()
                both = own_u[d, kk] + xrecv[level, d, kk].astype(f32)
                zsend[level, d, kk] = both.astype(bf)
                landed[d, kk] = remote(
                    zsend.at[level, d, kk], zrecv.at[level, d, kk], z_peer(d)
                )
        need("rhs%d" % (level + 1), "rhs%dc" % (level + 1))
        for kk in range(2):
            arrivals[0, kk].wait_recv()
            own_u[0, kk] += xrecv[level, 0, kk].astype(f32)
        own_u[0] = rhs_v[level] - own_u[0]
        for d in order[:2]:
            for kk in range(2):
                landed[d, kk].wait_recv()
                own_u[0, kk] -= zrecv[level, d, kk].astype(f32)
        gathers = []
        for kk in range(2):
            landed[order[2], kk].wait_recv()
            resid = own_u[0, kk] - zrecv[level, order[2], kk].astype(f32)
            r_v[level + 1, y * 2 + kk] = resid.astype(bf)
            gathers.append(to_y(r_v.at[level + 1], kk))
        return gathers

    for copy in first:
        copy.wait_recv()
    need("d0", "d0c")
    resid = full(r_v.at[0])
    gathers = []
    for kk in range(2):
        part = dot32(d_v[0, y * 2 + kk], resid)
        fwd_own[0, kk] = part
        f_v[0, y * 2 + kk] = part.astype(bf)
        gathers.append(to_y(f_v.at[0], kk))
    need("d1")
    d_y[1].start()
    need("loff0", "loff0c")
    for copy in gathers:
        copy.wait_recv()
    gathers = route_sum(0, full(f_v.at[0]))

    need("loff1", "loff1c", "d1c", "d2")
    d_y[2].start()
    relay_d(1)
    for copy in gathers:
        copy.wait_recv()
    d_relay[1].wait_recv()
    resid = full(r_v.at[1])
    for i in range(4):
        f_v[1, i] = dot32(d_v[1, i], resid).astype(bf)
    gathers = route_sum(1, full(f_v.at[1]))

    need("d2c")
    d_y[0].start()
    relay_d(2)
    resid = full(r_v.at[1])
    for kk in range(2):
        fwd_own[1, kk] = dot32(d_v[1, y * 2 + kk], resid)
    for copy in gathers:
        copy.wait_recv()
    d_relay[2].wait_recv()
    resid = full(r_v.at[2])
    for i in range(4):
        f_v[2, i] = dot32(d_v[2, i], resid).astype(bf)

    stores = []

    def finish(level, sols):
        for kk in range(2):
            out_v[level, kk] = sols[kk].T
        copy = pltpu.make_async_copy(
            out_v.at[level, k], out_hbm.at[level, :, lanes], local_sem.at[16 + level]
        )
        copy.start()
        away = remote(out_v.at[level, 1 - k], out_hbm.at[level, :, lanes], core_peer)
        stores.append((copy, away))

    from_x = {}
    from_z = {}

    def share(level, kk, sol_t):
        up_v[level, 0, kk] = sol_t.astype(bf)
        own_up = up_v.at[level, 0, kk]
        from_x[level, 0, kk] = remote(own_up, upx_v.at[level, 0, kk], x_peer)
        for d in ZS:
            from_z[level, d, kk] = remote(own_up, up_v.at[level, d, kk], z_peer(d))

    sols = []
    for kk in range(2):
        sols.append(
            lax.dot_general(
                full(f_v.at[2]),
                columns(2, y * 2 + kk),
                (((0,), (0,)), ((), ())),
                preferred_element_type=f32,
            )
        )
        share(1, kk, sols[kk])
    for level in (1, 0):
        finish(level + 1, sols)
        acc[...] = jnp.zeros((half, width), f32)
        at = pl.multiple_of(y * 2 * rows, 2 * rows)
        acc[:, pl.ds(at, 2 * rows)] = -(fwd_own[level].reshape(2 * rows, half).T)

        def gain(buf, kk, zt, xt):
            acc[...] += dot32(buf[...], link_rows(level, kk, zt, xt))

        for kk in range(2):
            gain(up_v.at[level, 0, kk], kk, z, x)
        for d, kk in STEPS:
            from_z[level, d, kk].wait_recv()
            from_x[level, d, kk] = remote(
                up_v.at[level, d, kk], upx_v.at[level, d, kk], x_peer
            )
            gain(up_v.at[level, d, kk], kk, z_at(NZ - d), x)
        if level == 0:
            relay_d(0)
        for d, kk in ((0, 0), (0, 1)) + STEPS:
            from_x[level, d, kk].wait_recv()
            gain(upx_v.at[level, d, kk], kk, z_at(NZ - d), 1 - x)
        if level == 0:
            need("d0c")
            d_relay[0].wait_recv()
        v_bf = acc[...].astype(bf)
        across = []
        for kk in range(2):
            ysend[level, kk] = dot32(v_bf, columns(level, (1 - y) * 2 + kk)).astype(bf)
            across.append(remote(ysend.at[level, kk], yrecv.at[level, kk], y_peer))
        mine = [dot32(v_bf, columns(level, y * 2 + kk)) for kk in range(2)]
        sols = []
        for kk in range(2):
            across[kk].wait_recv()
            sols.append(-(mine[kk] + yrecv[level, kk].astype(f32)))
            if level == 1:
                share(0, kk, sols[kk])
    finish(0, sols)
    for copy, away in stores:
        away.wait_recv()
        copy.wait()
    for copy in sent:
        copy.wait_send()


def fused_body(rhs, dinv, loff, targets):
    levels, rows, count = rhs.shape
    width = dinv.shape[2]
    links = targets.shape[1]
    half = count // 2
    bf = jnp.bfloat16
    f32 = jnp.float32
    any_space = pl.BlockSpec(memory_space=pl.ANY)
    pair = (2, rows, half)
    pair_t = (2, half, rows)
    return pl.pallas_call(
        fused_kernel,
        out_shape=jax.ShapeDtypeStruct(rhs.shape, f32),
        in_specs=[pl.BlockSpec(memory_space=pltpu.SMEM)] + [any_space] * 4,
        out_specs=any_space,
        scratch_shapes=[
            pltpu.VMEM((rows, count), f32),
            pltpu.VMEM((levels - 1,) + pair, f32),
            pltpu.VMEM((levels, 4, rows, width), bf),
            pltpu.VMEM((2, links, BLK, width), bf),
            pltpu.VMEM((2, links, BLK, width), bf),
            pltpu.VMEM((levels, 4, rows, half), bf),
            pltpu.VMEM((levels, 4, rows, half), bf),
            pltpu.VMEM((rows, half), bf),
            pltpu.VMEM((levels - 1,) + pair, f32),
            pltpu.VMEM((4,) + pair, f32),
            pltpu.VMEM((levels - 1, 4) + pair, bf),
            pltpu.VMEM((levels - 1, 4) + pair, bf),
            pltpu.VMEM((levels - 1, 4) + pair, bf),
            pltpu.VMEM((levels - 1, 4) + pair, bf),
            pltpu.VMEM((levels - 1, 4) + pair_t, bf),
            pltpu.VMEM((levels - 1, 4) + pair_t, bf),
            pltpu.VMEM((half, width), f32),
            pltpu.VMEM((levels - 1,) + pair_t, bf),
            pltpu.VMEM((levels - 1,) + pair_t, bf),
            pltpu.VMEM((levels,) + pair, f32),
            pltpu.VMEM((levels - 1, links), jnp.int32),
            pltpu.SMEM((levels - 1, links), jnp.int32),
            pltpu.SMEM((levels - 1, 2, links), jnp.int32),
            pltpu.SemaphoreType.DMA((20,)),
            pltpu.SemaphoreType.DMA((SENDS,)),
            pltpu.SemaphoreType.DMA((SENDS,)),
        ],
        compiler_params=pltpu.CompilerParams(
            collective_id=0, has_side_effects=True, vmem_limit_bytes=60 * 1024 * 1024
        ),
    )(targets, targets, rhs, dinv, loff.reshape(levels - 1, links, BLK, width))


def solution(mesh):
    in_specs = (
        P(None, ("snode", "col"), None),
        P(None, ("snode", "col"), None),
        P(None, ("snode", "col"), None),
        P(None, ("snode", "col")),
    )
    out_specs = P(None, ("snode", "col"), None)
    fits = mesh.shape["snode"] == 2 * NZ and mesh.shape["col"] == 4
    return jax.shard_map(
        fused_body if fits else body,
        mesh=mesh,
        in_specs=in_specs,
        out_specs=out_specs,
        check_vma=False,
    )
```

time: 103 us -> 100 us (0.971)
  the two profiles are of different devices: /device:TPU:16 before, /device:TPU:0 now
where the time goes in v2:
time: 100 us; the launch traced here: 99.2 us
  Pallas kernels  97.1 us (97%)
  local copies, waits for them, and re-layouts  2.06 us (2%)
    pallas_call x1, Pallas kernels, fused_body(): pl.pallas_call(fused_kernel, out_shape=jax.ShapeDtypeStruct(rhs.shape, f3...  97.1 us
    unnamed x1, local copies, waits for them, and re-layouts  2.06 us

profile of v2, /device:TPU:0, one launch (start us, length us, event | category | flops | bytes accessed | tf_op | source)
XLA Modules:
  0.0 99.2 jit_solution(17256330891180579602)
XLA Ops:
  0.0 97.1 %shard_map.46 = f32[3,256,256]{2,1,0:T(8,128)} custom-call(s32[2,16]{1,0:T(2,128)} %targets_hbm.1, s32[2,16]{1,0:T(2,128)} %targets_hbm.1, f32[3,256,256]{2,1,0:T(8,128)} %rhs_hbm.1, bf16[3,256,1024]{2,1,0:T(8,128)(2,1)} %dinv_hbm.1, bf16[2,16,128,1024]{3,2,1,0:T(8,128)(2,1)} %bitcast.1), custom_call_target="tpu_custom_call" | custom-call | tf_op jit(solution)/shard_map/pallas_call | solution.py:465
  97.1 2.1 %copy.6 = f32[3,256,256]{2,1,0:T(8,128)} copy(f32[3,256,256]{2,1,0:T(8,128)} %shard_map.46) | data formatting | bytes 1572864

commit v3 on v2

--- a/solution.py
+++ b/solution.py
@@ -107,9 +107,10 @@
 NZ = 4
 MESH_ID = pl.DeviceIdType.MESH
 SENDS = 96
-ZS = (2, 1, 3)
-STEPS = tuple((d, kk) for kk in range(2) for d in (2, 1, 3))
-RSO = (2, 1, 3, 0)
+ZS = (1, 3, 2)
+STEPS = ((1, 0), (3, 0), (1, 1), (3, 1), (2, 0), (2, 1))
+RSEQ = tuple((d, kk) for d in (2, 1, 3, 0) for kk in range(2))
+ZSEQ = tuple((d, kk) for d in (2, 1, 3) for kk in range(2))
 
 
 def dot32(a, b):
@@ -293,44 +294,35 @@
     for level in range(2):
         invert(level, 1 - k, peer_links)
 
-    order = RSO
-
     def route_sum(level, fwd_bf):
         arrivals = {}
-        for d in order:
-            for kk in range(2):
-                part = dot32(link_rows(level, kk, z_at(d), 1 - x), fwd_bf)
-                xsend[level, d, kk] = part.astype(bf)
-                arrivals[d, kk] = remote(
-                    xsend.at[level, d, kk], xrecv.at[level, d, kk], x_peer
-                )
-        for d in order:
-            for kk in range(2):
-                own_u[d, kk] = dot32(link_rows(level, kk, z_at(d), x), fwd_bf)
+        for d, kk in RSEQ:
+            part = dot32(link_rows(level, kk, z_at(d), 1 - x), fwd_bf)
+            xsend[level, d, kk] = part.astype(bf)
+            arrivals[d, kk] = remote(xsend.at[level, d, kk], xrecv.at[level, d, kk], x_peer)
+        for d, kk in RSEQ:
+            own_u[d, kk] = dot32(link_rows(level, kk, z_at(d), x), fwd_bf)
+        need("rhs%d" % (level + 1), "rhs%dc" % (level + 1))
         landed = {}
-        for d in order[:3]:
-            for kk in range(2):
-                arrivals[d, kk].wait_recv()
-                both = own_u[d, kk] + xrecv[level, d, kk].astype(f32)
-                zsend[level, d, kk] = both.astype(bf)
-                landed[d, kk] = remote(
-                    zsend.at[level, d, kk], zrecv.at[level, d, kk], z_peer(d)
-                )
-        need("rhs%d" % (level + 1), "rhs%dc" % (level + 1))
-        for kk in range(2):
-            arrivals[0, kk].wait_recv()
-            own_u[0, kk] += xrecv[level, 0, kk].astype(f32)
-        own_u[0] = rhs_v[level] - own_u[0]
-        for d in order[:2]:
-            for kk in range(2):
-                landed[d, kk].wait_recv()
-                own_u[0, kk] -= zrecv[level, d, kk].astype(f32)
+        for d, kk in RSEQ:
+            arrivals[d, kk].wait_recv()
+            both = own_u[d, kk] + xrecv[level, d, kk].astype(f32)
+            if d == 0:
+                own_u[0, kk] = rhs_v[level, kk] - both
+                continue
+            zsend[level, d, kk] = both.astype(bf)
+            landed[d, kk] = remote(zsend.at[level, d, kk], zrecv.at[level, d, kk], z_peer(d))
         gathers = []
-        for kk in range(2):
-            landed[order[2], kk].wait_recv()
-            resid = own_u[0, kk] - zrecv[level, order[2], kk].astype(f32)
-            r_v[level + 1, y * 2 + kk] = resid.astype(bf)
-            gathers.append(to_y(r_v.at[level + 1], kk))
+        left = [3, 3]
+        for d, kk in ZSEQ:
+            landed[d, kk].wait_recv()
+            left[kk] -= 1
+            resid = own_u[0, kk] - zrecv[level, d, kk].astype(f32)
+            if left[kk]:
+                own_u[0, kk] = resid
+            else:
+                r_v[level + 1, y * 2 + kk] = resid.astype(bf)
+                gathers.append(to_y(r_v.at[level + 1], kk))
         return gathers
 
     for copy in first:
@@ -376,15 +368,15 @@
 
     stores = []
 
-    def finish(level, sols):
-        for kk in range(2):
-            out_v[level, kk] = sols[kk].T
-        copy = pltpu.make_async_copy(
-            out_v.at[level, k], out_hbm.at[level, :, lanes], local_sem.at[16 + level]
-        )
-        copy.start()
-        away = remote(out_v.at[level, 1 - k], out_hbm.at[level, :, lanes], core_peer)
-        stores.append((copy, away))
+    def finish(level, kk, sol_t):
+        if kk == 0:
+            src, dst = out_v.at[level], out_hbm.at[level, :, lanes]
+            copy = pltpu.make_async_copy(src.at[k], dst, local_sem.at[16 + level])
+            stores.append((copy, describe(src.at[1 - k], dst, core_peer)))
+        out_v[level, kk] = sol_t.T
+        copy, away = stores[-1]
+        pl.when(k == kk)(copy.start)
+        pl.when(k != kk)(away.start)
 
     from_x = {}
     from_z = {}
@@ -408,7 +400,8 @@
         )
         share(1, kk, sols[kk])
     for level in (1, 0):
-        finish(level + 1, sols)
+        for kk in range(2):
+            finish(level + 1, kk, sols[kk])
         acc[...] = jnp.zeros((half, width), f32)
         at = pl.multiple_of(y * 2 * rows, 2 * rows)
         acc[:, pl.ds(at, 2 * rows)] = -(fwd_own[level].reshape(2 * rows, half).T)
@@ -444,7 +437,8 @@
             sols.append(-(mine[kk] + yrecv[level, kk].astype(f32)))
             if level == 1:
                 share(0, kk, sols[kk])
-    finish(0, sols)
+            else:
+                finish(0, kk, sols[kk])
     for copy, away in stores:
         away.wait_recv()
         copy.wait()

time: 100 us -> 96.8 us (0.968)
  Pallas kernels: 97.1 us -> 94.6 us
    pallas_call x1, Pallas kernels: 97.1 us -> 94.6 us  [fused_body(): pl.pallas_call(fused_kernel, out_shape=jax.ShapeDtypeStruct(rhs.shape, f3...]
where the time goes in v3:
time: 96.8 us; the launch traced here: 96.6 us
  Pallas kernels  94.6 us (98%)
  local copies, waits for them, and re-layouts  2.06 us (2%)
    pallas_call x1, Pallas kernels, fused_body(): pl.pallas_call(fused_kernel, out_shape=jax.ShapeDtypeStruct(rhs.shape, f3...  94.6 us
    unnamed x1, local copies, waits for them, and re-layouts  2.06 us

profile of v3, /device:TPU:0, one launch (start us, length us, event | category | flops | bytes accessed | tf_op | source)
XLA Modules:
  0.0 96.6 jit_solution(12500714310724285429)
XLA Ops:
  0.0 94.6 %shard_map.46 = f32[3,256,256]{2,1,0:T(8,128)} custom-call(s32[2,16]{1,0:T(2,128)} %targets_hbm.1, s32[2,16]{1,0:T(2,128)} %targets_hbm.1, f32[3,256,256]{2,1,0:T(8,128)} %rhs_hbm.1, bf16[3,256,1024]{2,1,0:T(8,128)(2,1)} %dinv_hbm.1, bf16[2,16,128,1024]{3,2,1,0:T(8,128)(2,1)} %bitcast.1), custom_call_target="tpu_custom_call" | custom-call | tf_op jit(solution)/shard_map/pallas_call | solution.py:459
  94.6 2.1 %copy.6 = f32[3,256,256]{2,1,0:T(8,128)} copy(f32[3,256,256]{2,1,0:T(8,128)} %shard_map.46) | data formatting | bytes 1572864

commit v4 on v3

--- a/solution.py
+++ b/solution.py
@@ -106,7 +106,10 @@
 
 NZ = 4
 MESH_ID = pl.DeviceIdType.MESH
-SENDS = 96
+SENDS = 110
+SLOTS = 48
+PA = 2
+PR = 1
 ZS = (1, 3, 2)
 STEPS = ((1, 0), (3, 0), (1, 1), (3, 1), (2, 0), (2, 1))
 RSEQ = tuple((d, kk) for d in (2, 1, 3, 0) for kk in range(2))
@@ -212,19 +215,24 @@
     pl.semaphore_wait(barrier, len(peers))
 
     sent = []
+    slots = []
+    free = set(range(SLOTS))
     pushed = {}
 
     def describe(src, dst, peer):
         at = len(sent)
+        slot = min(free)
+        free.remove(slot)
         copy = pltpu.make_async_remote_copy(
             src_ref=src,
             dst_ref=dst,
-            send_sem=send_sem.at[at],
+            send_sem=send_sem.at[slot],
             recv_sem=recv_sem.at[at],
             device_id=peer,
             device_id_type=MESH_ID,
         )
         sent.append(copy)
+        slots.append(slot)
         return copy
 
     def remote(src, dst, peer):
@@ -237,6 +245,11 @@
 
     def to_y(buf, kk):
         return remote(buf.at[y * 2 + kk], buf.at[y * 2 + kk], y_peer)
+
+    def pieces(src, dst, peer, count):
+        size = src.shape[0] // count
+        cuts = [pl.ds(at * size, size) for at in range(count)]
+        return [(cut, remote(src.at[cut], dst.at[cut], peer)) for cut in cuts]
 
     def full(buf):
         return buf[...].reshape(4 * rows, half)
@@ -285,6 +298,24 @@
         d_y[level].wait_recv()
         d_relay[level].start()
 
+    base = len(sent)
+    stores = []
+    settled = set()
+    late = {id(d_y[0]), id(d_relay[0])}
+
+    def settle(copies, outs):
+        final = copies is sent
+        for copy in copies:
+            if id(copy) not in settled and (final or id(copy) not in late):
+                settled.add(id(copy))
+                copy.wait_send()
+                free.add(slots[[other is copy for other in sent].index(True)])
+        for copy, away in outs:
+            if id(copy) not in settled:
+                settled.add(id(copy))
+                copy.wait()
+                away.wait_recv()
+
     for level in range(2):
         invert(level, k, targets_ref)
     need("links")
@@ -295,34 +326,43 @@
         invert(level, 1 - k, peer_links)
 
     def route_sum(level, fwd_bf):
+        mark = len(sent)
         arrivals = {}
         for d, kk in RSEQ:
             part = dot32(link_rows(level, kk, z_at(d), 1 - x), fwd_bf)
             xsend[level, d, kk] = part.astype(bf)
-            arrivals[d, kk] = remote(xsend.at[level, d, kk], xrecv.at[level, d, kk], x_peer)
+            arrivals[d, kk] = pieces(
+                xsend.at[level, d, kk], xrecv.at[level, d, kk], x_peer, PR
+            )
         for d, kk in RSEQ:
             own_u[d, kk] = dot32(link_rows(level, kk, z_at(d), x), fwd_bf)
         need("rhs%d" % (level + 1), "rhs%dc" % (level + 1))
+        settle((list(pushed.values()) if level else first) + sent[base:mark], [])
         landed = {}
         for d, kk in RSEQ:
-            arrivals[d, kk].wait_recv()
-            both = own_u[d, kk] + xrecv[level, d, kk].astype(f32)
-            if d == 0:
-                own_u[0, kk] = rhs_v[level, kk] - both
-                continue
-            zsend[level, d, kk] = both.astype(bf)
-            landed[d, kk] = remote(zsend.at[level, d, kk], zrecv.at[level, d, kk], z_peer(d))
+            landed[d, kk] = []
+            for cut, copy in arrivals[d, kk]:
+                copy.wait_recv()
+                both = own_u[d, kk, cut] + xrecv[level, d, kk, cut].astype(f32)
+                if d == 0:
+                    own_u[0, kk, cut] = rhs_v[level, kk, cut] - both
+                    continue
+                zsend[level, d, kk, cut] = both.astype(bf)
+                src, dst = zsend.at[level, d, kk, cut], zrecv.at[level, d, kk, cut]
+                landed[d, kk].append((cut, remote(src, dst, z_peer(d))))
         gathers = []
         left = [3, 3]
         for d, kk in ZSEQ:
-            landed[d, kk].wait_recv()
             left[kk] -= 1
-            resid = own_u[0, kk] - zrecv[level, d, kk].astype(f32)
-            if left[kk]:
-                own_u[0, kk] = resid
-            else:
-                r_v[level + 1, y * 2 + kk] = resid.astype(bf)
-                gathers.append(to_y(r_v.at[level + 1], kk))
+            for cut, copy in landed[d, kk]:
+                copy.wait_recv()
+                resid = own_u[0, kk, cut] - zrecv[level, d, kk, cut].astype(f32)
+                if left[kk]:
+                    own_u[0, kk, cut] = resid
+                else:
+                    r_v[level + 1, y * 2 + kk, cut] = resid.astype(bf)
+                    row = r_v.at[level + 1, y * 2 + kk, cut]
+                    gathers.append(remote(row, row, y_peer))
         return gathers
 
     for copy in first:
@@ -366,8 +406,6 @@
     for i in range(4):
         f_v[2, i] = dot32(d_v[2, i], resid).astype(bf)
 
-    stores = []
-
     def finish(level, kk, sol_t):
         if kk == 0:
             src, dst = out_v.at[level], out_hbm.at[level, :, lanes]
@@ -384,10 +422,11 @@
     def share(level, kk, sol_t):
         up_v[level, 0, kk] = sol_t.astype(bf)
         own_up = up_v.at[level, 0, kk]
-        from_x[level, 0, kk] = remote(own_up, upx_v.at[level, 0, kk], x_peer)
+        from_x[level, 0, kk] = [remote(own_up, upx_v.at[level, 0, kk], x_peer)]
         for d in ZS:
-            from_z[level, d, kk] = remote(own_up, up_v.at[level, d, kk], z_peer(d))
-
+            from_z[level, d, kk] = pieces(own_up, up_v.at[level, d, kk], z_peer(d), PA)
+
+    mark = len(sent)
     sols = []
     for kk in range(2):
         sols.append(
@@ -411,16 +450,23 @@
 
         for kk in range(2):
             gain(up_v.at[level, 0, kk], kk, z, x)
+        if level == 0:
+            settle(sent[:before], stores[:-1])
+        else:
+            settle(sent[base:mark] + [d_y[1], d_relay[1]], [])
         for d, kk in STEPS:
-            from_z[level, d, kk].wait_recv()
-            from_x[level, d, kk] = remote(
-                up_v.at[level, d, kk], upx_v.at[level, d, kk], x_peer
-            )
+            from_x[level, d, kk] = []
+            for cut, copy in from_z[level, d, kk]:
+                copy.wait_recv()
+                src, dst = up_v.at[level, d, kk, cut], upx_v.at[level, d, kk, cut]
+                from_x[level, d, kk].append(remote(src, dst, x_peer))
             gain(up_v.at[level, d, kk], kk, z_at(NZ - d), x)
         if level == 0:
             relay_d(0)
+            settle(sent[:-1], [])
         for d, kk in ((0, 0), (0, 1)) + STEPS:
-            from_x[level, d, kk].wait_recv()
+            for copy in from_x[level, d, kk]:
+                copy.wait_recv()
             gain(upx_v.at[level, d, kk], kk, z_at(NZ - d), 1 - x)
         if level == 0:
             need("d0c")
@@ -432,6 +478,7 @@
             across.append(remote(ysend.at[level, kk], yrecv.at[level, kk], y_peer))
         mine = [dot32(v_bf, columns(level, y * 2 + kk)) for kk in range(2)]
         sols = []
+        before = len(sent)
         for kk in range(2):
             across[kk].wait_recv()
             sols.append(-(mine[kk] + yrecv[level, kk].astype(f32)))
@@ -439,11 +486,7 @@
                 share(0, kk, sols[kk])
             else:
                 finish(0, kk, sols[kk])
-    for copy, away in stores:
-        away.wait_recv()
-        copy.wait()
-    for copy in sent:
-        copy.wait_send()
+    settle(sent, stores)
 
 
 def fused_body(rhs, dinv, loff, targets):
@@ -486,7 +529,7 @@
             pltpu.SMEM((levels - 1, links), jnp.int32),
             pltpu.SMEM((levels - 1, 2, links), jnp.int32),
             pltpu.SemaphoreType.DMA((20,)),
-            pltpu.SemaphoreType.DMA((SENDS,)),
+            pltpu.SemaphoreType.DMA((SLOTS,)),
             pltpu.SemaphoreType.DMA((SENDS,)),
         ],
         compiler_params=pltpu.CompilerParams(

time: 96.8 us -> 95.8 us (0.990)
  Pallas kernels: 94.6 us -> 93.5 us
    pallas_call x1, Pallas kernels: 94.6 us -> 93.5 us  [fused_body(): pl.pallas_call(fused_kernel, out_shape=jax.ShapeDtypeStruct(rhs.shape, f3...]
where the time goes in v4:
time: 95.8 us; the launch traced here: 95.6 us
  Pallas kernels  93.5 us (98%)
  local copies, waits for them, and re-layouts  2.06 us (2%)
    pallas_call x1, Pallas kernels, fused_body(): pl.pallas_call(fused_kernel, out_shape=jax.ShapeDtypeStruct(rhs.shape, f3...  93.5 us
    unnamed x1, local copies, waits for them, and re-layouts  2.06 us

profile of v4, /device:TPU:0, one launch (start us, length us, event | category | flops | bytes accessed | tf_op | source)
XLA Modules:
  0.0 95.6 jit_solution(1826139638343321237)
XLA Ops:
  0.0 93.5 %shard_map.46 = f32[3,256,256]{2,1,0:T(8,128)} custom-call(s32[2,16]{1,0:T(2,128)} %targets_hbm.1, s32[2,16]{1,0:T(2,128)} %targets_hbm.1, f32[3,256,256]{2,1,0:T(8,128)} %rhs_hbm.1, bf16[3,256,1024]{2,1,0:T(8,128)(2,1)} %dinv_hbm.1, bf16[2,16,128,1024]{3,2,1,0:T(8,128)(2,1)} %bitcast.1), custom_call_target="tpu_custom_call" | custom-call | tf_op jit(solution)/shard_map/pallas_call | solution.py:502
  93.5 2.1 %copy.6 = f32[3,256,256]{2,1,0:T(8,128)} copy(f32[3,256,256]{2,1,0:T(8,128)} %shard_map.46) | data formatting | bytes 1572864

commit v5 on v4

--- a/solution.py
+++ b/solution.py
@@ -106,7 +106,7 @@
 
 NZ = 4
 MESH_ID = pl.DeviceIdType.MESH
-SENDS = 110
+SENDS = 94
 SLOTS = 48
 PA = 2
 PR = 1
@@ -424,7 +424,9 @@
         own_up = up_v.at[level, 0, kk]
         from_x[level, 0, kk] = [remote(own_up, upx_v.at[level, 0, kk], x_peer)]
         for d in ZS:
-            from_z[level, d, kk] = pieces(own_up, up_v.at[level, d, kk], z_peer(d), PA)
+            from_z[level, d, kk] = pieces(
+                own_up, up_v.at[level, d, kk], z_peer(d), PA if d == 2 else 1
+            )
 
     mark = len(sent)
     sols = []

time: 95.8 us -> 95.9 us (level)
  no operation moved by 1% of the time
where the time goes in v5:
time: 95.9 us; the launch traced here: 95.8 us
  Pallas kernels  93.7 us (98%)
  local copies, waits for them, and re-layouts  2.06 us (2%)
    pallas_call x1, Pallas kernels, fused_body(): pl.pallas_call(fused_kernel, out_shape=jax.ShapeDtypeStruct(rhs.shape, f3...  93.7 us
    unnamed x1, local copies, waits for them, and re-layouts  2.06 us

profile of v5, /device:TPU:0, one launch (start us, length us, event | category | flops | bytes accessed | tf_op | source)
XLA Modules:
  0.0 95.8 jit_solution(8064468659238326041)
XLA Ops:
  0.0 93.7 %shard_map.46 = f32[3,256,256]{2,1,0:T(8,128)} custom-call(s32[2,16]{1,0:T(2,128)} %targets_hbm.1, s32[2,16]{1,0:T(2,128)} %targets_hbm.1, f32[3,256,256]{2,1,0:T(8,128)} %rhs_hbm.1, bf16[3,256,1024]{2,1,0:T(8,128)(2,1)} %dinv_hbm.1, bf16[2,16,128,1024]{3,2,1,0:T(8,128)(2,1)} %bitcast.1), custom_call_target="tpu_custom_call" | custom-call | tf_op jit(solution)/shard_map/pallas_call | solution.py:504
  93.7 2.1 %copy.6 = f32[3,256,256]{2,1,0:T(8,128)} copy(f32[3,256,256]{2,1,0:T(8,128)} %shard_map.46) | data formatting | bytes 1572864
